TPU v7x, 32 devices: a whole 2x2x4 slice. The times are simulated.
32 devices in a mesh: dp: 2 (over x), ctx: 4 (over z), tp: 4 (over y, core).
Axes of the slice: x: 2, y: 2, z: 4, core: 2. Of those that a mesh axis runs over, the one named last changes fastest.
Arguments:
- hidden_in: bfloat16 [2, 2, 2048, 768], P(None, 'dp', 'ctx'), may hold values from -6 to 6
- prefix: int32 [2, 2], P(None, 'dp'), may hold values from 204 to 1024
- block_order: int32 [8], replicated, may hold values from 0 to 7, each once
- qkv_weight: bfloat16 [3, 768, 768], P(None, 'dp', 'tp'), may hold values from -0.3125 to 0.3125
- out_weight: bfloat16 [768, 768], P('tp', 'dp'), may hold values from -2.5 to 2.5
- up_weight: bfloat16 [768, 3072], P('dp', 'tp'), may hold values from -0.21875 to 0.21875
- down_weight: bfloat16 [3072, 768], P('tp', 'dp'), may hold values from -0.4375 to 0.4375
- ln_gains: bfloat16 [2, 768], P(None, 'dp'), may hold values from 0.5 to 1.5
- ln_shifts: bfloat16 [2, 768], P(None, 'dp'), may hold values from -2 to 2
- cotangent: bfloat16 [2, 2, 2048, 768], P(None, 'dp', 'ctx'), may hold values from -6 to 6
Outputs:
- block_out: bfloat16 [2, 2, 2048, 768], P(None, 'dp', 'ctx')
- grad_in: float32 [2, 2, 2048, 768], P(None, 'dp', 'ctx')
- grad_qkv: float32 [3, 768, 768], P(None, 'dp', 'tp')
- grad_out: float32 [768, 768], P('tp', 'dp')
- grad_up: float32 [768, 3072], P('dp', 'tp')
- grad_down: float32 [3072, 768], P('tp', 'dp')
- grad_gains: float32 [2, 768], P(None, 'dp')
- grad_shifts: float32 [2, 768], P(None, 'dp')
Inputs may be any that keep to these rules, and one draw needn't show every extreme that they name: `prefix`: leading positions of each sequence that all of its queries see. `block_order`: each of the 2 * 4 block numbers appears once.
All inputs are finite; a program needn't handle non-finite values.
Results may differ from a plain program's by a relative error of at most 0.012.
The roundings to bfloat16 on the way count: a program that leaves them out, or rounds other values in their place, can miss the bound.
Values may be sent and summed in bfloat16 or wider, within the bound.
A program may use at most 128 MiB of HBM per device.

v0:
```python
import jax
import jax.numpy as jnp
from jax import lax
from jax.sharding import PartitionSpec as P

HEAD_DIM = 64
DEPTH = 12
EPS = 1e-05
GELU_C = 0.7978845608028654
GELU_A = 0.044715
NEG = -1e30
ROW_BLOCK = 512


def apply_layer_norm(values, norm_gain, norm_shift):
    row_mean = jnp.mean(values, axis=1, keepdims=True)
    centered_input = values - row_mean
    inverse_deviation = lax.rsqrt(
        jnp.mean(centered_input * centered_input, axis=1, keepdims=True) + EPS
    )
    normalized_input = centered_input * inverse_deviation
    return (normalized_input * norm_gain + norm_shift, normalized_input, inverse_deviation)


def norm_backward(normed_gradient, normalized_input, inverse_deviation, norm_gain):
    scaled_gradient = normed_gradient * norm_gain
    return inverse_deviation * (
        scaled_gradient
        - jnp.mean(scaled_gradient, axis=1, keepdims=True)
        - normalized_input * jnp.mean(scaled_gradient * normalized_input, axis=1, keepdims=True)
    )


def gelu_value(u):
    return 0.5 * u * (1.0 + jnp.tanh(GELU_C * (u + GELU_A * u * u * u)))


def gelu_slope(u):
    inner = jnp.tanh(GELU_C * (u + GELU_A * u * u * u))
    return 0.5 * (1.0 + inner) + 0.5 * u * (1.0 - inner * inner) * GELU_C * (
        1.0 + 3.0 * GELU_A * u * u
    )


def block_positions(block_order, rows, half):
    slots = jnp.arange(block_order.shape[0], dtype=jnp.int32)
    picked = jnp.where((rows // half)[:, None] == slots[None, :], block_order[None, :], 0)
    return jnp.sum(picked, axis=1) * half + rows % half


def fetch_weights(qkv_weight, out_weight, up_weight, down_weight, ln_gains, ln_shifts):
    return (
        lax.all_gather(qkv_weight, "dp", axis=1, tiled=True),
        lax.all_gather(out_weight, "dp", axis=1, tiled=True),
        lax.all_gather(up_weight, "dp", axis=0, tiled=True),
        lax.all_gather(down_weight, "dp", axis=1, tiled=True),
        lax.all_gather(ln_gains, "dp", axis=1, tiled=True),
        lax.all_gather(ln_shifts, "dp", axis=1, tiled=True),
    )


def body(
    hidden_in,
    prefix,
    block_order,
    qkv_weight,
    out_weight,
    up_weight,
    down_weight,
    ln_gains,
    ln_shifts,
    cotangent,
):
    micro = hidden_in.shape[0]
    tokens = hidden_in.shape[2]
    width = hidden_in.shape[3]
    local_width = qkv_weight.shape[2]
    head_dim = HEAD_DIM
    local_heads = local_width // head_dim
    seq_len = tokens * lax.axis_size("ctx")
    half = tokens // 2
    branch = DEPTH ** (-0.5)
    scale = head_dim ** (-0.5)
    block_rows = min(tokens, ROW_BLOCK)
    blocks = tokens // block_rows
    query_rows = lax.axis_index("ctx") * tokens + jnp.arange(tokens, dtype=jnp.int32)
    key_rows = jnp.arange(seq_len, dtype=jnp.int32)
    query_pos = block_positions(block_order, query_rows, half)
    key_pos = block_positions(block_order, key_rows, half)
    acc_qkv = jnp.zeros((3, width, local_width), jnp.float32)
    acc_out = jnp.zeros((local_width, width), jnp.float32)
    acc_up = jnp.zeros((width, up_weight.shape[1]), jnp.float32)
    acc_down = jnp.zeros((down_weight.shape[0], width), jnp.float32)
    acc_gains = jnp.zeros((2, width), jnp.float32)
    acc_shifts = jnp.zeros((2, width), jnp.float32)
    results = []
    input_gradient_list = []
    for index in range(micro):
        full = fetch_weights(qkv_weight, out_weight, up_weight, down_weight, ln_gains, ln_shifts)
        qkv_full, out_full, up_full, down_full, gains_full, shifts_full = full
        norm_gains = gains_full.astype(jnp.float32)
        norm_shifts = shifts_full.astype(jnp.float32)
        input_rows = hidden_in[index, 0].astype(jnp.float32)
        allowed = (key_pos[None, :] <= query_pos[:, None]) | (key_pos[None, :] < prefix[index, 0])
        first_normed, normalized_first1, inverse_deviation1 = apply_layer_norm(
            input_rows, norm_gains[0], norm_shifts[0]
        )
        h1 = first_normed.astype(jnp.bfloat16)
        qkv = jnp.einsum("td,kde->kte", h1, qkv_full, preferred_element_type=jnp.float32).astype(
            jnp.bfloat16
        )
        keys_flat, values_flat = (
            lax.all_gather(qkv[1], "ctx", axis=0, tiled=True),
            lax.all_gather(qkv[2], "ctx", axis=0, tiled=True),
        )
        keys = keys_flat.reshape(seq_len, local_heads, head_dim)
        values = values_flat.reshape(seq_len, local_heads, head_dim)
        q_blocks = qkv[0].reshape(blocks, block_rows, local_heads, head_dim)
        a_blocks = allowed.reshape(blocks, block_rows, seq_len)

        def attend(item):
            q_blk, allow_blk = item
            scores = (
                jnp.einsum("qhd,khd->hqk", q_blk, keys, preferred_element_type=jnp.float32) * scale
            )
            scores = jnp.where(allow_blk[None], scores, NEG)
            top = jnp.max(scores, axis=2, keepdims=True)
            expd = jnp.exp(scores - top)
            total = jnp.sum(expd, axis=2, keepdims=True)
            prob = (expd / total).astype(jnp.bfloat16)
            mixed = jnp.einsum("hqk,khd->qhd", prob, values, preferred_element_type=jnp.float32)
            return (mixed.astype(jnp.bfloat16), (top + jnp.log(total))[:, :, 0])

        heads_out, logsum = lax.map(attend, (q_blocks, a_blocks))
        heads = heads_out.reshape(tokens, local_width)
        attn_part = jnp.dot(heads, out_full, preferred_element_type=jnp.float32)
        attn = lax.psum(attn_part, "tp")
        middle_state = input_rows + branch * attn
        second_normed, normalized_second2, inverse_deviation2 = apply_layer_norm(
            middle_state, norm_gains[1], norm_shifts[1]
        )
        h2 = second_normed.astype(jnp.bfloat16)
        up = jnp.dot(h2, up_full, preferred_element_type=jnp.float32)
        act = gelu_value(up).astype(jnp.bfloat16)
        mlp_part = jnp.dot(act, down_full, preferred_element_type=jnp.float32)
        mlp = lax.psum(mlp_part, "tp")
        results.append((middle_state + branch * mlp).astype(jnp.bfloat16))
        qkv_full, out_full, up_full, down_full, gains_full, shifts_full = fetch_weights(
            qkv_weight, out_weight, up_weight, down_weight, ln_gains, ln_shifts
        )
        upstream_gradient = cotangent[index, 0].astype(jnp.float32)
        d_mlp = (branch * upstream_gradient).astype(jnp.bfloat16)
        grad_down = jnp.einsum("tf,td->fd", act, d_mlp, preferred_element_type=jnp.float32)
        d_act = jnp.einsum("td,fd->tf", d_mlp, down_full, preferred_element_type=jnp.float32)
        d_up = (d_act * gelu_slope(up)).astype(jnp.bfloat16)
        grad_up = jnp.einsum("td,tf->df", h2, d_up, preferred_element_type=jnp.float32)
        n2_back = jnp.einsum("tf,df->td", d_up, up_full, preferred_element_type=jnp.float32)
        second_norm_gradient = lax.psum(n2_back, "tp")
        middle_gradient = upstream_gradient + norm_backward(
            second_norm_gradient, normalized_second2, inverse_deviation2, norm_gains[1]
        )
        d_attn = (branch * middle_gradient).astype(jnp.bfloat16)
        grad_out = jnp.einsum("te,td->ed", heads, d_attn, preferred_element_type=jnp.float32)
        d_heads = jnp.einsum(
            "td,ed->te", d_attn, out_full, preferred_element_type=jnp.float32
        ).astype(jnp.bfloat16)
        dh_blocks = d_heads.reshape(blocks, block_rows, local_heads, head_dim)

        def attend_back(carry, item):
            key_sum, value_sum = carry
            q_blk, allow_blk, lse_blk, dh_blk = item
            scores = (
                jnp.einsum("qhd,khd->hqk", q_blk, keys, preferred_element_type=jnp.float32) * scale
            )
            scores = jnp.where(allow_blk[None], scores, NEG)
            prob = jnp.exp(scores - lse_blk[:, :, None])
            prob_low = prob.astype(jnp.bfloat16)
            d_prob = jnp.einsum("qhd,khd->hqk", dh_blk, values, preferred_element_type=jnp.float32)
            d_scores = (prob * (d_prob - jnp.sum(prob * d_prob, axis=2, keepdims=True))).astype(
                jnp.bfloat16
            )
            d_query = (
                jnp.einsum("hqk,khd->qhd", d_scores, keys, preferred_element_type=jnp.float32)
                * scale
            ).astype(jnp.bfloat16)
            key_sum = (
                key_sum
                + jnp.einsum("hqk,qhd->khd", d_scores, q_blk, preferred_element_type=jnp.float32)
                * scale
            )
            value_sum = value_sum + jnp.einsum(
                "hqk,qhd->khd", prob_low, dh_blk, preferred_element_type=jnp.float32
            )
            return ((key_sum, value_sum), d_query)

        zero_kv = jnp.zeros((seq_len, local_heads, head_dim), jnp.float32)
        (key_sum, value_sum), d_query = lax.scan(
            attend_back, (zero_kv, zero_kv), (q_blocks, a_blocks, logsum, dh_blocks)
        )
        d_keys, d_values = (
            lax.psum_scatter(
                key_sum.reshape(seq_len, local_width), "ctx", scatter_dimension=0, tiled=True
            ),
            lax.psum_scatter(
                value_sum.reshape(seq_len, local_width), "ctx", scatter_dimension=0, tiled=True
            ),
        )
        d_qkv = jnp.stack(
            [
                d_query.reshape(tokens, local_width),
                d_keys.astype(jnp.bfloat16),
                d_values.astype(jnp.bfloat16),
            ]
        )
        grad_qkv = jnp.einsum("td,kte->kde", h1, d_qkv, preferred_element_type=jnp.float32)
        n1_back = jnp.einsum("kte,kde->td", d_qkv, qkv_full, preferred_element_type=jnp.float32)
        first_norm_gradient = lax.psum(n1_back, "tp")
        input_gradient_list.append(
            middle_gradient
            + norm_backward(
                first_norm_gradient, normalized_first1, inverse_deviation1, norm_gains[0]
            )
        )
        acc_gains = acc_gains + jnp.stack(
            [
                jnp.sum(first_norm_gradient * normalized_first1, axis=0),
                jnp.sum(second_norm_gradient * normalized_second2, axis=0),
            ]
        )
        acc_shifts = acc_shifts + jnp.stack(
            [jnp.sum(first_norm_gradient, axis=0), jnp.sum(second_norm_gradient, axis=0)]
        )
        acc_qkv = acc_qkv + grad_qkv
        acc_out = acc_out + grad_out
        acc_up = acc_up + grad_up
        acc_down = acc_down + grad_down
    whole_qkv, whole_out, whole_up, whole_down, whole_gains, whole_shifts = lax.psum(
        (acc_qkv, acc_out, acc_up, acc_down, acc_gains, acc_shifts), "ctx"
    )
    owned = (
        lax.psum_scatter(whole_qkv, "dp", scatter_dimension=1, tiled=True),
        lax.psum_scatter(whole_out, "dp", scatter_dimension=1, tiled=True),
        lax.psum_scatter(whole_up, "dp", scatter_dimension=0, tiled=True),
        lax.psum_scatter(whole_down, "dp", scatter_dimension=1, tiled=True),
        lax.psum_scatter(whole_gains, "dp", scatter_dimension=1, tiled=True),
        lax.psum_scatter(whole_shifts, "dp", scatter_dimension=1, tiled=True),
    )
    block_out = jnp.stack(results)[:, None]
    grad_in = jnp.stack(input_gradient_list)[:, None]
    return (block_out, grad_in, owned[0], owned[1], owned[2], owned[3], owned[4], owned[5])


def solution(mesh):
    in_specs = (
        P(None, "dp", "ctx", None),
        P(None, "dp"),
        P(),
        P(None, "dp", "tp"),
        P("tp", "dp"),
        P("dp", "tp"),
        P("tp", "dp"),
        P(None, "dp"),
        P(None, "dp"),
        P(None, "dp", "ctx", None),
    )
    out_specs = (
        P(None, "dp", "ctx", None),
        P(None, "dp", "ctx", None),
        P(None, "dp", "tp"),
        P("tp", "dp"),
        P("dp", "tp"),
        P("tp", "dp"),
        P(None, "dp"),
        P(None, "dp"),
    )
    return jax.shard_map(body, mesh=mesh, in_specs=in_specs, out_specs=out_specs, check_vma=False)
```

profile of v0, /device:TPU:0, one launch (start us, length us, event | category | flops | bytes accessed | tf_op | source)
XLA Modules:
  0.0 766.6 jit_solution(9417610063547408217)
XLA Ops:
  10.2 5.5 all_gather.20
  15.7 4.5 all_gather.21
  20.3 1.7 convert_reduce_fusion.1
  22.8 5.9 all_gather.49
  28.7 9.4 %all_gather.22 = bf16[3,768,192]{1,2,0:T(8,128)(2,1)S(1)} all-gather(bf16[3,384,192]{1,2,0:T(8,128)(2,1)S(1)} %copy-done.43), channel_id=1, replica_groups=mesh['dp'=2,'ctx'=4,'tp'=4] {'dp'}, dimensions={1}, use_global_device_ids=true | all-gather | bytes 1327104 | tf_op jit(solution)/shard_map/all_gather | solution.py:53
  39.8 19.5 %all-gather.3 = bf16[1,2048,192]{1,2,0:T(8,128)(2,1)S(1)} all-gather(bf16[1,512,192]{1,2,0:T(8,128)(2,1)S(1)} %get-tuple-element.187), channel_id=5, replica_groups=mesh['dp'=2,'ctx'=4,'tp'=4] {'ctx'}, dimensions={1}, use_global_device_ids=true | all-gather | bytes 983040 | tf_op jit(solution)/shard_map/all_gather | solution.py:113
  59.3 17.9 %all-gather.2 = bf16[1,2048,192]{1,2,0:T(8,128)(2,1)S(1)} all-gather(bf16[1,512,192]{1,2,0:T(8,128)(2,1)S(1)} %get-tuple-element.189), channel_id=4, replica_groups=mesh['dp'=2,'ctx'=4,'tp'=4] {'ctx'}, dimensions={1}, use_global_device_ids=true | all-gather | bytes 983040 | tf_op jit(solution)/shard_map/all_gather | solution.py:114
  78.2 17.1 %all-gather.1 = bf16[1,2048,192]{1,2,0:T(8,128)(2,1)S(1)} all-gather(bf16[1,512,192]{1,2,0:T(8,128)(2,1)S(1)} %get-tuple-element.184), channel_id=3, replica_groups=mesh['dp'=2,'ctx'=4,'tp'=4] {'ctx'}, dimensions={1}, use_global_device_ids=true | all-gather | bytes 983040 | tf_op jit(solution)/shard_map/all_gather | solution.py:113
  95.3 15.7 %all-gather = bf16[1,2048,192]{1,2,0:T(8,128)(2,1)S(1)} all-gather(bf16[1,512,192]{1,2,0:T(8,128)(2,1)S(1)} %get-tuple-element.186), channel_id=2, replica_groups=mesh['dp'=2,'ctx'=4,'tp'=4] {'ctx'}, dimensions={1}, use_global_device_ids=true | all-gather | bytes 983040 | tf_op jit(solution)/shard_map/all_gather | solution.py:114
  112.3 2.2 compare_or_fusion.1
  114.5 2.7 fusion.124
  117.2 1.9 fusion
  119.1 2.6 copy-done
  121.7 3.6 fusion.65
  125.4 1.6 fusion.125
  126.9 2.7 fusion.123
  129.6 1.9 fusion.1
  131.5 2.6 copy-done.1
  134.1 3.1 fusion.64
  137.2 1.6 fusion.126
  140.2 68.0 %all-reduce.14.cloned.1.call-done = (f32[512,768]{1,0:T(8,128)}, f32[512,768]{1,0:T(8,128)}) async-done(((f32[512,768]{1,0:T(8,128)}, f32[512,768]{1,0:T(8,128)}), (f32[512,768]{1,0:T(8,128)}, f32[512,768]{1,0:T(8,128)})) %all-reduce.14.cloned.1.call-update) | async-done | bytes 3145744 | tf_op jit(solution)/shard_map/psum | solution.py:137
  208.2 2.4 fusion.116
  211.8 3.9 fusion.114
  215.7 2.1 fusion.115
  217.8 3.6 fusion.56
  223.0 2.0 fusion.128
  224.9 2.0 fusion.127
  227.0 68.7 %all-reduce.12.cloned.1.call-done = (f32[512,768]{1,0:T(8,128)}, f32[512,768]{1,0:T(8,128)}) async-done(((f32[512,768]{1,0:T(8,128)}, f32[512,768]{1,0:T(8,128)}), (f32[512,768]{1,0:T(8,128)}, f32[512,768]{1,0:T(8,128)})) %all-reduce.12.cloned.1.call-update) | async-done | bytes 3145744 | tf_op jit(solution)/shard_map/psum | solution.py:158
  295.7 3.8 multiply_reduce_fusion.3
  300.0 2.1 convert_add_fusion.1
  303.7 7.9 %fusion.6 = f32[3,64,2048]{2,1,0:T(8,128)} fusion(bf16[512,3,64]{0,2,1:T(8,128)(2,1)S(1)} %bitcast.237, f32[3,512,2048]{2,1,0:T(8,128)} %copy-done, f32[3,512]{1,0:T(4,128)S(1)} %log_add_fusion.1), kind=kOutput, calls=%fused_computation.17 | convolution fusion | flops 408944640 | bytes 14358528 | tf_op jit(solution)/shard_map/while/body/eval_jaxpr/hqk,qhd->khd/dot_general | solution.py:191
  311.9 1.8 convolution_convert_fusion
  313.8 8.2 %fusion.4 = f32[3,64,2048]{2,1,0:T(8,128)} fusion(bf16[512,3,64]{0,2,1:T(8,128)(2,1)S(1)} %bitcast.239, f32[3,512,2048]{2,1,0:T(8,128)} %copy-done.1, f32[3,512]{1,0:T(4,128)S(1)} %log_add_fusion), kind=kOutput, calls=%fused_computation.16 | convolution fusion | flops 408944640 | bytes 14358528 | tf_op jit(solution)/shard_map/while/body/eval_jaxpr/hqk,qhd->khd/dot_general | solution.py:191
  322.9 6.6 multiply_reduce_fusion
  329.5 6.5 multiply_convert_fusion
  336.0 2.9 convolution_multiply_fusion
  339.9 6.6 multiply_reduce_fusion.1
  346.6 6.4 multiply_convert_fusion.1
  353.0 2.9 convolution_multiply_fusion.1
  356.6 4.1 fusion.112
  360.7 3.9 fusion.111
  364.6 5.6 fusion.63
  370.2 2.7 fusion.62
  374.0 10.4 %reduce-scatter.21.cloned.1.call-done = f32[512,192]{0,1:T(8,128)} async-done(((f32[2048,192]{0,1:T(8,128)}), f32[512,192]{0,1:T(8,128)}) %reduce-scatter.21.cloned.1.call-update) | async-done | bytes 393232 | tf_op jit(solution)/shard_map/reduce_scatter | solution.py:204
  385.4 35.6 %reduce-scatter.19.cloned.1.call-done = f32[512,192]{0,1:T(8,128)} async-done(((f32[2048,192]{0,1:T(8,128)}), f32[512,192]{0,1:T(8,128)}) %reduce-scatter.19.cloned.1.call-update) | async-done | bytes 393232 | tf_op jit(solution)/shard_map/reduce_scatter | solution.py:201
  422.7 3.2 convolution_bitcast_fusion
  426.0 31.6 %reduce-scatter.15.cloned.1.call-done = f32[512,192]{0,1:T(8,128)} async-done(((f32[2048,192]{0,1:T(8,128)}), f32[512,192]{0,1:T(8,128)}) %reduce-scatter.15.cloned.1.call-update) | async-done | bytes 393232 | tf_op jit(solution)/shard_map/reduce_scatter | solution.py:201
  459.3 3.3 convolution_bitcast_fusion.1
  463.5 1.8 fusion.80
  466.7 3.1 fusion.113
  469.8 2.5 convolution_add_fusion.1
  472.4 2.9 fusion.73
  475.3 2.6 convolution_add_fusion
  478.9 2.0 fusion.69
  481.0 2.1 add_bitcast_fusion
  483.8 97.4 %all-reduce.10.cloned.1.call-done = (f32[512,768]{1,0:T(8,128)}, f32[512,768]{1,0:T(8,128)}, f32[512,768]{1,0:T(8,128)}, f32[512,768]{1,0:T(8,128)}) async-done(((f32[512,768]{1,0:T(8,128)}, f32[512,768]{1,0:T(8,128)}, f32[512,768]{1,0:T(8,128)}, f32[512,768]{1,0:T(8,128)}), (f32[512,768]{1,0:T(8,128)}, f32[512,768]{1,0:T(8,128)}, f32[512,768]{1,0:T(8,128)}, ...) | async-done | bytes 6291472 | tf_op jit(solution)/shard_map/psum | solution.py:146
  581.2 2.9 fusion.44
  586.8 2.2 fusion.66
  593.8 1.9 maximum_bitcast_fusion
  595.7 5.8 reduce-scatter.33.cloned.1.call-done
  602.5 15.0 %reduce-scatter.31.cloned.1.call-done = f32[384,2]{1,0:T(8,128)} async-done(((f32[768,2]{1,0:T(8,128)}), f32[384,2]{1,0:T(8,128)}) %reduce-scatter.31.cloned.1.call-update) | async-done | bytes 3088
  618.5 12.6 %all-reduce.3 = (f32[2,384]{1,0:T(2,128)}, f32[2,384]{1,0:T(2,128)}) all-reduce(f32[2,384]{1,0:T(2,128)S(1)} %copy.25, f32[2,384]{1,0:T(2,128)S(1)} %copy.27), channel_id=1, replica_groups=mesh['dp'=2,'ctx'=4,'tp'=4] {'ctx'}, use_global_device_ids=true, to_apply=%region_48.49 | all-reduce | flops 1536 | bytes 12288 | tf_op jit(solution)/shard_map/psum | solution.py:237
  631.1 122.6 %all-reduce.16.cloned.1.call-done = (f32[3,384,192]{1,2,0:T(8,128)}, f32[192,384]{1,0:T(8,128)}, f32[384,768]{1,0:T(8,128)}, f32[768,384]{1,0:T(8,128)}) async-done(((f32[3,384,192]{1,2,0:T(8,128)}, f32[192,384]{1,0:T(8,128)}, f32[384,768]{1,0:T(8,128)}, f32[768,384]{1,0:T(8,128)}), (f32[3,384,192]{1,2,0:T(8,128)}, f32[192,384]{1,0:T(8,128)}, f32[384,768]{1,0:T(8,128)}, ...) | async-done | bytes 3538960 | tf_op jit(solution)/shard_map/psum | solution.py:237
  753.8 2.2 copy.40
  (273 shorter events, 37.6 us)
Async XLA Ops:
  8.0 14.0 %copy-start.4 = (bf16[2,1,512,768]{3,2,1,0:T(8,128)(2,1)S(1)}, bf16[2,1,512,768]{3,2,1,0:T(8,128)(2,1)}, u32[]{:S(2)}) copy-start(bf16[2,1,512,768]{3,2,1,0:T(8,128)(2,1)} %param.10) | copy-start | bytes 4718596
  8.0 200.2 %all-reduce.14.cloned.1.call-start = ((), (), s32[]{:S(2)}) async-start(), calls=%async_computation.24 | async-start | bytes 6291456 | tf_op jit(solution)/shard_map/psum | solution.py:137
  20.2 56.9 %copy-start.73 = (f32[768]{0:T(1024)}, f32[768]{0:T(1024)S(1)}, u32[]{:S(2)}) copy-start(f32[768]{0:T(1024)S(1)} %get-tuple-element.159) | copy-start | bytes 9220
  20.3 195.5 %copy-start.67 = (f32[768]{0:T(1024)}, f32[768]{0:T(1024)S(1)}, u32[]{:S(2)}) copy-start(f32[768]{0:T(1024)S(1)} %get-tuple-element.158) | copy-start | bytes 9220
  20.3 8.4 %copy-start.43 = (bf16[3,384,192]{1,2,0:T(8,128)(2,1)S(1)}, bf16[3,384,192]{1,2,0:T(8,128)(2,1)}, u32[]{:S(2)}) copy-start(bf16[3,384,192]{1,2,0:T(8,128)(2,1)} %param.13) | copy-start | bytes 1327108
  22.0 16.1 %copy-start.54 = (f32[512]{0:T(512)}, f32[512]{0:T(512)S(1)}, u32[]{:S(2)}) copy-start(f32[512]{0:T(512)S(1)} %broadcast_multiply_fusion.9) | copy-start | bytes 6148
  22.7 54.5 %copy-start.60 = (f32[512]{0:T(512)}, f32[512]{0:T(512)S(1)}, u32[]{:S(2)}) copy-start(f32[512]{0:T(512)S(1)} %add_rsqrt_fusion.3) | copy-start | bytes 6148
  22.7 16.3 %copy-start.62 = (f32[512]{0:T(512)}, f32[512]{0:T(512)S(1)}, u32[]{:S(2)}) copy-start(f32[512]{0:T(512)S(1)} %add_rsqrt_fusion.1) | copy-start | bytes 6148
  38.1 39.1 %copy-start.32 = (bf16[3,768,192]{1,2,0:T(8,128)(2,1)}, bf16[3,768,192]{1,2,0:T(8,128)(2,1)S(1)}, u32[]{:S(2)}) copy-start(bf16[3,768,192]{1,2,0:T(8,128)(2,1)S(1)} %all_gather.22) | copy-start | bytes 2654212
  59.3 67.6 %copy-start.17 = (bf16[1,2048,192]{1,2,0:T(8,128)(2,1)}, bf16[1,2048,192]{1,2,0:T(8,128)(2,1)S(1)}, u32[]{:S(2)}) copy-start(bf16[1,2048,192]{1,2,0:T(8,128)(2,1)S(1)} %all-gather.3) | copy-start | bytes 2359300
  77.2 54.3 %copy-start.16 = (bf16[1,2048,192]{1,2,0:T(8,128)(2,1)}, bf16[1,2048,192]{1,2,0:T(8,128)(2,1)S(1)}, u32[]{:S(2)}) copy-start(bf16[1,2048,192]{1,2,0:T(8,128)(2,1)S(1)} %all-gather.2) | copy-start | bytes 2359300
  78.2 36.3 %copy-start.39 = (bf16[1,512,192]{1,2,0:T(8,128)(2,1)}, bf16[1,512,192]{1,2,0:T(8,128)(2,1)S(1)}, u32[]{:S(2)}) copy-start(bf16[1,512,192]{1,2,0:T(8,128)(2,1)S(1)} %get-tuple-element.185) | copy-start | bytes 589828
  95.3 21.9 %copy-start.19 = (bf16[1,2048,192]{1,2,0:T(8,128)(2,1)}, bf16[1,2048,192]{1,2,0:T(8,128)(2,1)S(1)}, u32[]{:S(2)}) copy-start(bf16[1,2048,192]{1,2,0:T(8,128)(2,1)S(1)} %all-gather.1) | copy-start | bytes 2359300
  111.0 8.1 %copy-start.15 = (bf16[1,2048,192]{1,2,0:T(8,128)(2,1)}, bf16[1,2048,192]{1,2,0:T(8,128)(2,1)S(1)}, u32[]{:S(2)}) copy-start(bf16[1,2048,192]{1,2,0:T(8,128)(2,1)S(1)} %all-gather) | copy-start | bytes 2359300
  117.2 4.5 copy-start
  125.3 4.3 copy-start.35
  129.6 4.5 copy-start.1
  138.8 73.0 %all-gather.7.cloned.1.call-start = ((), (), s32[]{:S(2)}) async-start(), calls=%async_computation.10 | async-start | bytes 1769472 | tf_op jit(solution)/shard_map/all_gather | solution.py:55
  139.3 78.5 %all-gather.9.cloned.1.call-start = ((), (), s32[]{:S(2)}) async-start(), calls=%async_computation.11 | async-start | bytes 1769472 | tf_op jit(solution)/shard_map/all_gather | solution.py:56
  139.9 155.8 %all-reduce.12.cloned.1.call-start = ((), (), s32[]{:S(2)}) async-start(), calls=%async_computation.23 | async-start | bytes 6291456 | tf_op jit(solution)/shard_map/psum | solution.py:158
  210.6 88.9 %copy-start.56 = (f32[512]{0:T(512)}, f32[512]{0:T(512)S(1)}, u32[]{:S(2)}) copy-start(f32[512]{0:T(512)S(1)} %broadcast_multiply_fusion.10) | copy-start | bytes 6148
  211.8 87.8 %copy-start.58 = (f32[512]{0:T(512)}, f32[512]{0:T(512)S(1)}, u32[]{:S(2)}) copy-start(f32[512]{0:T(512)S(1)} %add_rsqrt_fusion) | copy-start | bytes 6148
  211.8 87.8 %copy-start.65 = (f32[512]{0:T(512)}, f32[512]{0:T(512)S(1)}, u32[]{:S(2)}) copy-start(f32[512]{0:T(512)S(1)} %add_rsqrt_fusion.2) | copy-start | bytes 6148
  211.8 3.9 copy-start.78
  217.8 3.6 copy-start.25
  217.8 3.6 copy-start.76
  217.8 3.6 copy-start.81
  221.4 3.5 copy-start.80
  226.9 146.0 %reduce-scatter.17.cloned.1.call-start = ((), (), s32[]{:S(2)}) async-start(), calls=%async_computation.13 | async-start | bytes 1966080 | tf_op jit(solution)/shard_map/reduce_scatter | solution.py:204
  295.7 3.9 copy-start.6
  295.7 3.9 copy-start.13
  295.7 3.9 copy-start.14
  295.7 4.3 copy-start.26
  303.7 7.9 %copy-start.21 = (bf16[512,192]{0,1:T(8,128)(2,1)}, bf16[512,192]{0,1:T(8,128)(2,1)S(1)}, u32[]{:S(2)}) copy-start(bf16[512,192]{0,1:T(8,128)(2,1)S(1)} %convolution_convert_fusion.1) | copy-start | bytes 589828
  311.6 72.8 %reduce-scatter.21.cloned.1.call-start = ((), (), s32[]{:S(2)}) async-start(), calls=%async_computation.15 | async-start | bytes 1966080 | tf_op jit(solution)/shard_map/reduce_scatter | solution.py:204
  313.8 8.2 %copy-start.23 = (bf16[512,192]{0,1:T(8,128)(2,1)}, bf16[512,192]{0,1:T(8,128)(2,1)S(1)}, u32[]{:S(2)}) copy-start(bf16[512,192]{0,1:T(8,128)(2,1)S(1)} %convolution_convert_fusion) | copy-start | bytes 589828
  322.0 99.0 %reduce-scatter.19.cloned.1.call-start = ((), (), s32[]{:S(2)}) async-start(), calls=%async_computation.14 | async-start | bytes 1966080 | tf_op jit(solution)/shard_map/reduce_scatter | solution.py:201
  329.5 6.5 copy-start.42
  336.0 3.1 copy-start.2
  339.0 118.6 %reduce-scatter.15.cloned.1.call-start = ((), (), s32[]{:S(2)}) async-start(), calls=%async_computation.12 | async-start | bytes 1966080 | tf_op jit(solution)/shard_map/reduce_scatter | solution.py:201
  346.5 6.5 copy-start.40
  353.0 3.2 copy-start.3
  356.3 224.9 %all-reduce.10.cloned.1.call-start = ((), (), s32[]{:S(2)}) async-start(), calls=%async_computation.22 | async-start | bytes 12582912 | tf_op jit(solution)/shard_map/psum | solution.py:146
  356.6 4.1 copy-start.77
  356.6 13.6 %slice-start = ((s8[6291456]{0:T(1024)(128)(4,1)}), s8[4194304]{0:T(1024)(128)(4,1)S(1)}, s32[]{:S(2)}) async-start(s8[6291456]{0:T(1024)(128)(4,1)} %bitcast.223), calls=%async_computation.26 | async-start | bytes 8388608
  360.7 3.9 copy-start.18
  360.7 9.5 %slice-start.1 = ((s8[6291456]{0:T(1024)(128)(4,1)}), s8[2097152]{0:T(1024)(128)(4,1)S(1)}, s32[]{:S(2)}) async-start(s8[6291456]{0:T(1024)(128)(4,1)} %bitcast.223), calls=%async_computation.27 | async-start | bytes 4194304
  364.6 5.6 copy-start.20
  374.0 84.7 %copy-start.45 = (bf16[1,512,192]{1,2,0:T(8,128)(2,1)}, bf16[1,512,192]{1,2,0:T(8,128)(2,1)S(1)}, u32[]{:S(2)}) copy-start(bf16[1,512,192]{1,2,0:T(8,128)(2,1)S(1)} %convert_bitcast_fusion.6) | copy-start | bytes 589828
  385.4 40.5 %copy-start.47 = (bf16[1,512,192]{1,2,0:T(8,128)(2,1)}, bf16[1,512,192]{1,2,0:T(8,128)(2,1)S(1)}, u32[]{:S(2)}) copy-start(bf16[1,512,192]{1,2,0:T(8,128)(2,1)S(1)} %convert_bitcast_fusion.4) | copy-start | bytes 589828
  462.6 123.6 %reduce-scatter.25.cloned.1.call-start = ((), (), s32[]{:S(2)}) async-start(), calls=%async_computation.17 | async-start | bytes 884736 | tf_op jit(solution)/shard_map/reduce_scatter | solution.py:242
  466.6 3.2 copy-start.59
  466.6 119.7 %reduce-scatter.27.cloned.1.call-start = ((), (), s32[]{:S(2)}) async-start(), calls=%async_computation.18 | async-start | bytes 3538944 | tf_op jit(solution)/shard_map/reduce_scatter | solution.py:243
  466.7 3.1 copy-start.34
  472.3 114.0 %reduce-scatter.29.cloned.1.call-start = ((), (), s32[]{:S(2)}) async-start(), calls=%async_computation.19 | async-start | bytes 3538944 | tf_op jit(solution)/shard_map/reduce_scatter | solution.py:244
  472.4 3.0 copy-start.27
  472.4 2.9 copy-start.82
  478.0 108.3 %reduce-scatter.23.cloned.1.call-start = ((), (), s32[]{:S(2)}) async-start(), calls=%async_computation.16 | async-start | bytes 2654208 | tf_op jit(solution)/shard_map/reduce_scatter | solution.py:241
  483.1 98.1 %copy-start.64 = (f32[512]{0:T(512)S(1)}, f32[512]{0:T(512)}, u32[]{:S(2)}) copy-start(f32[512]{0:T(512)} %copy-done.62) | copy-start | bytes 6148
  483.1 118.4 %reduce-scatter.33.cloned.1.call-start = ((), (), s32[]{:S(2)}) async-start(), calls=%async_computation.21 | async-start | bytes 589824
  585.1 32.4 %reduce-scatter.31.cloned.1.call-start = ((), (), s32[]{:S(2)}) async-start(), calls=%async_computation.20 | async-start | bytes 589824
  586.2 167.6 %all-reduce.16.cloned.1.call-start = ((), (), s32[]{:S(2)}) async-start(), calls=%async_computation.25 | async-start | bytes 7077888 | tf_op jit(solution)/shard_map/psum | solution.py:237
  589.4 3.2 copy-start.10
  753.8 3.0 copy-start.30
  (37 other events, 59.9 us)
Sparse Core Ops, SparseCore 0:
  138.9 69.2 all-reduce.13
  227.1 68.5 all-reduce.11
  462.7 118.4 all-reduce.9
Sparse Core Ops, SparseCore 1:
  140.8 23.4 all-gather.6
  165.7 22.6 all-gather.8
  311.7 35.5 reduce-scatter.16
  350.2 34.2 reduce-scatter.20
  386.7 34.2 reduce-scatter.18
  423.4 34.2 reduce-scatter.14
  466.7 14.0 reduce-scatter.24
  483.5 34.7 reduce-scatter.26
  520.3 34.7 reduce-scatter.28
  557.4 28.2 reduce-scatter.22
  588.3 13.1 reduce-scatter.32
  604.3 13.1 reduce-scatter.30
  620.0 133.7 all-reduce.15
where the time goes:
time: 775 us; the launch traced here: 767 us
  waiting for transfers between devices  457 us (59%)
  matrix products  110 us (14%)
  blocking collectives  108 us (14%)
  other arithmetic  46.1 us (6%)
  local copies, waits for them, and re-layouts  26.5 us (3%)
  between operations  17.2 us (2%)
    psum x1, waiting for transfers between devices, body(): lax.psum((acc_qkv, acc_out, acc_up, acc_down, acc_gains, acc_shifts), 'ctx')  123 us
    psum x1, waiting for transfers between devices, body(): mlp = lax.psum(mlp_part, 'tp')  97.4 us
    psum x1, waiting for transfers between devices, body(): second_norm_gradient = lax.psum(n2_back, 'tp')  68.7 us
    psum x1, waiting for transfers between devices, body(): attn = lax.psum(attn_part, 'tp')  68 us
    reduce_scatter x2, waiting for transfers between devices, body(): lax.psum_scatter(key_sum.reshape(seq_len, local_width), 'ctx', scatter_di...  67.2 us
    all_gather x2, blocking collectives, body(): lax.all_gather(qkv[1], 'ctx', axis=0, tiled=True)  36.6 us
    all_gather x2, blocking collectives, body(): lax.all_gather(qkv[2], 'ctx', axis=0, tiled=True)  33.6 us
    unnamed x178, local copies, waits for them, and re-layouts  24.3 us
  transfers between devices with their start and end apart: 16, of which 9 were waited for; matrix products, arithmetic and copies ran while one was open for 14% of the time, Pallas kernels for 0%

commit v1 on v0

--- a/solution.py
+++ b/solution.py
@@ -155,7 +155,7 @@
         d_up = (d_act * gelu_slope(up)).astype(jnp.bfloat16)
         grad_up = jnp.einsum("td,tf->df", h2, d_up, preferred_element_type=jnp.float32)
         n2_back = jnp.einsum("tf,df->td", d_up, up_full, preferred_element_type=jnp.float32)
-        second_norm_gradient = lax.psum(n2_back, "tp")
+        second_norm_gradient = jnp.sum(lax.all_gather(n2_back, "tp"), 0)
         middle_gradient = upstream_gradient + norm_backward(
             second_norm_gradient, normalized_second2, inverse_deviation2, norm_gains[1]
         )

time: 775 us -> 802 us (1.035)
  other arithmetic: 46.1 us -> 65 us
  starting transfers between devices: 1.62 us -> 12.6 us
    all_gather x0 -> x2, waiting for transfers between devices: none -> 70.5 us  [body(): second_norm_gradient = jnp.sum(lax.all_gather(n2_back, 'tp'), 0)]
    psum x1 -> x0, waiting for transfers between devices: 68.7 us -> none  [body(): second_norm_gradient = lax.psum(n2_back, 'tp')]
    reduce_sum x0 -> x4, other arithmetic: none -> 15.7 us  [the longest x2 9.03 us: body(): second_norm_gradient = jnp.sum(lax.all_gather(n2_back, 'tp'), 0)]
    all_gather x0 -> x2, starting transfers between devices: none -> 11.5 us  [body(): second_norm_gradient = jnp.sum(lax.all_gather(n2_back, 'tp'), 0)]
    unnamed x18 -> x19, waiting for transfers between devices: 22.5 us -> 23.5 us
    unnamed x178 -> x172, local copies, waits for them, and re-layouts: 24.3 us -> 24.1 us
  transfers between devices with their start and end apart: 16 -> 17, of which waited for: 9 -> 11; matrix products, arithmetic and copies ran while one was open for 14% -> 15% of each run, Pallas kernels for 0% -> 0%
where the time goes in v1:
time: 802 us; the launch traced here: 794 us
  waiting for transfers between devices  456 us (57%)
  matrix products  109 us (14%)
  blocking collectives  108 us (13%)
  other arithmetic  65 us (8%)
  local copies, waits for them, and re-layouts  26.3 us (3%)
  between operations  17.2 us (2%)
  starting transfers between devices  12.6 us (2%)
    psum x1, waiting for transfers between devices, body(): lax.psum((acc_qkv, acc_out, acc_up, acc_down, acc_gains, acc_shifts), 'ctx')  123 us
    psum x1, waiting for transfers between devices, body(): mlp = lax.psum(mlp_part, 'tp')  91.7 us
    all_gather x2, waiting for transfers between devices, body(): second_norm_gradient = jnp.sum(lax.all_gather(n2_back, 'tp'), 0)  70.5 us
    psum x1, waiting for transfers between devices, body(): attn = lax.psum(attn_part, 'tp')  68.2 us
    reduce_scatter x2, waiting for transfers between devices, body(): lax.psum_scatter(key_sum.reshape(seq_len, local_width), 'ctx', scatter_di...  67.2 us
    all_gather x2, blocking collectives, body(): lax.all_gather(qkv[1], 'ctx', axis=0, tiled=True)  36.6 us
    all_gather x2, blocking collectives, body(): lax.all_gather(qkv[2], 'ctx', axis=0, tiled=True)  33.6 us
    unnamed x172, local copies, waits for them, and re-layouts  24.1 us
  transfers between devices with their start and end apart: 17, of which 11 were waited for; matrix products, arithmetic and copies ran while one was open for 15% of the time, Pallas kernels for 0%

profile of v1, /device:TPU:0, one launch (start us, length us, event | category | flops | bytes accessed | tf_op | source)
XLA Modules:
  0.0 793.8 jit_solution(18335861244914604201)
XLA Ops:
  10.2 5.5 all_gather.56
  15.7 4.5 all_gather.57
  22.8 5.9 all_gather.61
  28.8 9.4 %all_gather.58 = bf16[3,768,192]{1,2,0:T(8,128)(2,1)S(1)} all-gather(bf16[3,384,192]{1,2,0:T(8,128)(2,1)S(1)} %copy-done.42), channel_id=1, replica_groups=mesh['dp'=2,'ctx'=4,'tp'=4] {'dp'}, dimensions={1}, use_global_device_ids=true | all-gather | bytes 1327104 | tf_op jit(solution)/shard_map/all_gather | solution.py:53
  39.8 19.5 %all-gather.3 = bf16[1,2048,192]{1,2,0:T(8,128)(2,1)S(1)} all-gather(bf16[1,512,192]{1,2,0:T(8,128)(2,1)S(1)} %get-tuple-element.183), channel_id=5, replica_groups=mesh['dp'=2,'ctx'=4,'tp'=4] {'ctx'}, dimensions={1}, use_global_device_ids=true | all-gather | bytes 983040 | tf_op jit(solution)/shard_map/all_gather | solution.py:113
  59.3 17.8 %all-gather.2 = bf16[1,2048,192]{1,2,0:T(8,128)(2,1)S(1)} all-gather(bf16[1,512,192]{1,2,0:T(8,128)(2,1)S(1)} %get-tuple-element.185), channel_id=4, replica_groups=mesh['dp'=2,'ctx'=4,'tp'=4] {'ctx'}, dimensions={1}, use_global_device_ids=true | all-gather | bytes 983040 | tf_op jit(solution)/shard_map/all_gather | solution.py:114
  78.2 17.1 %all-gather.1 = bf16[1,2048,192]{1,2,0:T(8,128)(2,1)S(1)} all-gather(bf16[1,512,192]{1,2,0:T(8,128)(2,1)S(1)} %get-tuple-element.180), channel_id=3, replica_groups=mesh['dp'=2,'ctx'=4,'tp'=4] {'ctx'}, dimensions={1}, use_global_device_ids=true | all-gather | bytes 983040 | tf_op jit(solution)/shard_map/all_gather | solution.py:113
  95.3 15.7 %all-gather = bf16[1,2048,192]{1,2,0:T(8,128)(2,1)S(1)} all-gather(bf16[1,512,192]{1,2,0:T(8,128)(2,1)S(1)} %get-tuple-element.182), channel_id=2, replica_groups=mesh['dp'=2,'ctx'=4,'tp'=4] {'ctx'}, dimensions={1}, use_global_device_ids=true | all-gather | bytes 983040 | tf_op jit(solution)/shard_map/all_gather | solution.py:114
  112.4 2.2 compare_or_fusion.1
  114.5 2.7 fusion.124
  117.2 1.9 fusion
  119.1 2.6 copy-done
  121.7 3.3 fusion.65
  126.7 2.7 fusion.123
  129.3 1.9 fusion.1
  131.3 2.7 copy-done.1
  133.9 3.1 fusion.64
  139.8 68.2 %all-reduce.10.cloned.1.call-done = (f32[512,768]{1,0:T(8,128)}, f32[512,768]{1,0:T(8,128)}) async-done(((f32[512,768]{1,0:T(8,128)}, f32[512,768]{1,0:T(8,128)}), (f32[512,768]{1,0:T(8,128)}, f32[512,768]{1,0:T(8,128)})) %all-reduce.10.cloned.1.call-update) | async-done | bytes 3145744 | tf_op jit(solution)/shard_map/psum | solution.py:137
  208.1 3.4 fusion.116
  211.8 3.3 fusion.115
  215.2 3.5 fusion.61
  219.6 2.0 fusion.128
  221.6 11.5 %all-gather.15.cloned.1.call-start = ((), (), s32[]{:S(2)}) async-start(), calls=%async_computation.16 | async-start | bytes 7864320 | tf_op jit(solution)/shard_map/all_gather | solution.py:158
  235.0 2.3 fusion.114
  239.7 2.0 fusion.127
  241.7 26.4 %all-gather.17.cloned.1.call-done = f32[2048,768]{1,0:T(8,128)} async-done(((f32[512,768]{1,0:T(8,128)}), f32[2048,768]{1,0:T(8,128)}) %all-gather.17.cloned.1.call-update) | async-done | bytes 6291472 | tf_op jit(solution)/shard_map/all_gather | solution.py:158
  268.2 4.5 reduce_sum.310
  272.7 44.0 %all-gather.15.cloned.1.call-done = f32[2048,768]{1,0:T(8,128)} async-done(((f32[512,768]{1,0:T(8,128)}), f32[2048,768]{1,0:T(8,128)}) %all-gather.15.cloned.1.call-update) | async-done | bytes 6291472 | tf_op jit(solution)/shard_map/all_gather | solution.py:158
  316.7 4.5 reduce_sum.304
  321.2 3.8 multiply_reduce_fusion.3
  325.5 2.1 convert_add_fusion.1
  329.2 8.0 %fusion.6 = f32[3,64,2048]{2,1,0:T(8,128)} fusion(bf16[512,3,64]{0,2,1:T(8,128)(2,1)S(1)} %bitcast.241, f32[3,512,2048]{2,1,0:T(8,128)} %copy-done, f32[3,512]{1,0:T(4,128)S(1)} %log_add_fusion.1), kind=kOutput, calls=%fused_computation.17 | convolution fusion | flops 408944640 | bytes 14358528 | tf_op jit(solution)/shard_map/while/body/eval_jaxpr/hqk,qhd->khd/dot_general | solution.py:191
  339.0 8.2 %fusion.4 = f32[3,64,2048]{2,1,0:T(8,128)} fusion(bf16[512,3,64]{0,2,1:T(8,128)(2,1)S(1)} %bitcast.243, f32[3,512,2048]{2,1,0:T(8,128)} %copy-done.1, f32[3,512]{1,0:T(4,128)S(1)} %log_add_fusion), kind=kOutput, calls=%fused_computation.16 | convolution fusion | flops 408944640 | bytes 14358528 | tf_op jit(solution)/shard_map/while/body/eval_jaxpr/hqk,qhd->khd/dot_general | solution.py:191
  348.1 6.6 multiply_reduce_fusion
  354.7 6.5 multiply_convert_fusion
  361.2 2.9 convolution_multiply_fusion
  365.3 6.6 multiply_reduce_fusion.1
  371.9 6.4 multiply_convert_fusion.1
  378.4 2.9 convolution_multiply_fusion.1
  381.9 4.1 fusion.112
  386.0 3.8 fusion.111
  389.8 5.6 fusion.63
  395.5 2.7 fusion.62
  399.2 10.6 %reduce-scatter.21.cloned.1.call-done = f32[512,192]{0,1:T(8,128)} async-done(((f32[2048,192]{0,1:T(8,128)}), f32[512,192]{0,1:T(8,128)}) %reduce-scatter.21.cloned.1.call-update) | async-done | bytes 393232 | tf_op jit(solution)/shard_map/reduce_scatter | solution.py:204
  410.9 35.6 %reduce-scatter.19.cloned.1.call-done = f32[512,192]{0,1:T(8,128)} async-done(((f32[2048,192]{0,1:T(8,128)}), f32[512,192]{0,1:T(8,128)}) %reduce-scatter.19.cloned.1.call-update) | async-done | bytes 393232 | tf_op jit(solution)/shard_map/reduce_scatter | solution.py:201
  448.1 3.3 convolution_bitcast_fusion
  451.4 31.6 %reduce-scatter.15.cloned.1.call-done = f32[512,192]{0,1:T(8,128)} async-done(((f32[2048,192]{0,1:T(8,128)}), f32[512,192]{0,1:T(8,128)}) %reduce-scatter.15.cloned.1.call-update) | async-done | bytes 393232 | tf_op jit(solution)/shard_map/reduce_scatter | solution.py:201
  484.7 3.3 convolution_bitcast_fusion.1
  488.6 2.7 fusion.113
  491.3 2.5 convolution_add_fusion.1
  493.9 2.9 fusion.73
  496.9 2.6 convolution_add_fusion
  503.9 2.0 fusion.69
  506.0 2.1 add_bitcast_fusion
  508.2 3.4 reduce_sum.323
  511.6 3.2 reduce_sum.321
  514.9 91.7 %all-reduce.8.cloned.1.call-done = (f32[512,768]{1,0:T(8,128)}, f32[512,768]{1,0:T(8,128)}, f32[512,768]{1,0:T(8,128)}, f32[512,768]{1,0:T(8,128)}) async-done(((f32[512,768]{1,0:T(8,128)}, f32[512,768]{1,0:T(8,128)}, f32[512,768]{1,0:T(8,128)}, f32[512,768]{1,0:T(8,128)}), (f32[512,768]{1,0:T(8,128)}, f32[512,768]{1,0:T(8,128)}, f32[512,768]{1,0:T(8,128)}, ...) | async-done | bytes 6291472 | tf_op jit(solution)/shard_map/psum | solution.py:146
  606.6 2.9 fusion.44
  613.0 2.9 fusion.66
  621.5 7.2 reduce-scatter.33.cloned.1.call-done
  629.8 15.0 %reduce-scatter.31.cloned.1.call-done = f32[384,2]{1,0:T(8,128)} async-done(((f32[768,2]{1,0:T(8,128)}), f32[384,2]{1,0:T(8,128)}) %reduce-scatter.31.cloned.1.call-update) | async-done | bytes 3088
  645.8 12.6 %all-reduce.2 = (f32[2,384]{1,0:T(2,128)}, f32[2,384]{1,0:T(2,128)}) all-reduce(f32[2,384]{1,0:T(2,128)S(1)} %copy.25, f32[2,384]{1,0:T(2,128)S(1)} %copy.27), channel_id=1, replica_groups=mesh['dp'=2,'ctx'=4,'tp'=4] {'ctx'}, use_global_device_ids=true, to_apply=%region_48.49 | all-reduce | flops 1536 | bytes 12288 | tf_op jit(solution)/shard_map/psum | solution.py:237
  658.4 122.6 %all-reduce.12.cloned.1.call-done = (f32[3,384,192]{1,2,0:T(8,128)}, f32[192,384]{1,0:T(8,128)}, f32[384,768]{1,0:T(8,128)}, f32[768,384]{1,0:T(8,128)}) async-done(((f32[3,384,192]{1,2,0:T(8,128)}, f32[192,384]{1,0:T(8,128)}, f32[384,768]{1,0:T(8,128)}, f32[768,384]{1,0:T(8,128)}), (f32[3,384,192]{1,2,0:T(8,128)}, f32[192,384]{1,0:T(8,128)}, f32[384,768]{1,0:T(8,128)}, ...) | async-done | bytes 3538960 | tf_op jit(solution)/shard_map/psum | solution.py:237
  781.0 2.2 copy.38
  (272 shorter events, 49.4 us)
Async XLA Ops:
  8.0 14.1 %copy-start.4 = (bf16[2,1,512,768]{3,2,1,0:T(8,128)(2,1)S(1)}, bf16[2,1,512,768]{3,2,1,0:T(8,128)(2,1)}, u32[]{:S(2)}) copy-start(bf16[2,1,512,768]{3,2,1,0:T(8,128)(2,1)} %param.10) | copy-start | bytes 4718596
  8.0 200.0 %all-reduce.10.cloned.1.call-start = ((), (), s32[]{:S(2)}) async-start(), calls=%async_computation.25 | async-start | bytes 6291456 | tf_op jit(solution)/shard_map/psum | solution.py:137
  15.7 61.5 %copy-start.53 = (f32[768]{0:T(1024)}, f32[768]{0:T(1024)S(1)}, u32[]{:S(2)}) copy-start(f32[768]{0:T(1024)S(1)} %get-tuple-element.155) | copy-start | bytes 9220
  20.3 56.9 %copy-start.70 = (f32[768]{0:T(1024)}, f32[768]{0:T(1024)S(1)}, u32[]{:S(2)}) copy-start(f32[768]{0:T(1024)S(1)} %get-tuple-element.157) | copy-start | bytes 9220
  20.3 214.6 %copy-start.66 = (f32[768]{0:T(1024)}, f32[768]{0:T(1024)S(1)}, u32[]{:S(2)}) copy-start(f32[768]{0:T(1024)S(1)} %get-tuple-element.156) | copy-start | bytes 9220
  20.3 8.5 %copy-start.42 = (bf16[3,384,192]{1,2,0:T(8,128)(2,1)S(1)}, bf16[3,384,192]{1,2,0:T(8,128)(2,1)}, u32[]{:S(2)}) copy-start(bf16[3,384,192]{1,2,0:T(8,128)(2,1)} %param.13) | copy-start | bytes 1327108
  22.0 55.1 %copy-start.55 = (f32[512]{0:T(512)}, f32[512]{0:T(512)S(1)}, u32[]{:S(2)}) copy-start(f32[512]{0:T(512)S(1)} %broadcast_multiply_fusion.11) | copy-start | bytes 6148
  22.1 16.1 %copy-start.57 = (f32[512]{0:T(512)}, f32[512]{0:T(512)S(1)}, u32[]{:S(2)}) copy-start(f32[512]{0:T(512)S(1)} %broadcast_multiply_fusion.9) | copy-start | bytes 6148
  22.7 54.5 %copy-start.59 = (f32[512]{0:T(512)}, f32[512]{0:T(512)S(1)}, u32[]{:S(2)}) copy-start(f32[512]{0:T(512)S(1)} %add_rsqrt_fusion.3) | copy-start | bytes 6148
  22.7 16.3 %copy-start.61 = (f32[512]{0:T(512)}, f32[512]{0:T(512)S(1)}, u32[]{:S(2)}) copy-start(f32[512]{0:T(512)S(1)} %add_rsqrt_fusion.1) | copy-start | bytes 6148
  38.1 39.1 %copy-start.31 = (bf16[3,768,192]{1,2,0:T(8,128)(2,1)}, bf16[3,768,192]{1,2,0:T(8,128)(2,1)S(1)}, u32[]{:S(2)}) copy-start(bf16[3,768,192]{1,2,0:T(8,128)(2,1)S(1)} %all_gather.58) | copy-start | bytes 2654212
  59.3 67.3 %copy-start.17 = (bf16[1,2048,192]{1,2,0:T(8,128)(2,1)}, bf16[1,2048,192]{1,2,0:T(8,128)(2,1)S(1)}, u32[]{:S(2)}) copy-start(bf16[1,2048,192]{1,2,0:T(8,128)(2,1)S(1)} %all-gather.3) | copy-start | bytes 2359300
  77.2 54.1 %copy-start.16 = (bf16[1,2048,192]{1,2,0:T(8,128)(2,1)}, bf16[1,2048,192]{1,2,0:T(8,128)(2,1)S(1)}, u32[]{:S(2)}) copy-start(bf16[1,2048,192]{1,2,0:T(8,128)(2,1)S(1)} %all-gather.2) | copy-start | bytes 2359300
  78.2 36.3 %copy-start.38 = (bf16[1,512,192]{1,2,0:T(8,128)(2,1)}, bf16[1,512,192]{1,2,0:T(8,128)(2,1)S(1)}, u32[]{:S(2)}) copy-start(bf16[1,512,192]{1,2,0:T(8,128)(2,1)S(1)} %get-tuple-element.181) | copy-start | bytes 589828
  95.3 21.9 %copy-start.19 = (bf16[1,2048,192]{1,2,0:T(8,128)(2,1)}, bf16[1,2048,192]{1,2,0:T(8,128)(2,1)S(1)}, u32[]{:S(2)}) copy-start(bf16[1,2048,192]{1,2,0:T(8,128)(2,1)S(1)} %all-gather.1) | copy-start | bytes 2359300
  111.0 8.1 %copy-start.15 = (bf16[1,2048,192]{1,2,0:T(8,128)(2,1)}, bf16[1,2048,192]{1,2,0:T(8,128)(2,1)S(1)}, u32[]{:S(2)}) copy-start(bf16[1,2048,192]{1,2,0:T(8,128)(2,1)S(1)} %all-gather) | copy-start | bytes 2359300
  117.2 4.5 copy-start
  125.1 4.3 copy-start.34
  129.3 4.6 copy-start.1
  138.6 73.2 %all-gather.11.cloned.1.call-start = ((), (), s32[]{:S(2)}) async-start(), calls=%async_computation.10 | async-start | bytes 1769472 | tf_op jit(solution)/shard_map/all_gather | solution.py:55
  139.2 76.0 %all-gather.13.cloned.1.call-start = ((), (), s32[]{:S(2)}) async-start(), calls=%async_computation.11 | async-start | bytes 1769472 | tf_op jit(solution)/shard_map/all_gather | solution.py:56
  139.8 128.4 %all-gather.17.cloned.1.call-start = ((), (), s32[]{:S(2)}) async-start(), calls=%async_computation.17 | async-start | bytes 7864320 | tf_op jit(solution)/shard_map/all_gather | solution.py:158
  215.2 4.4 copy-start.75
  221.6 95.1 %all-gather.15.cloned.1.call-start = ((), (), s32[]{:S(2)}) async-start(), calls=%async_computation.16 | async-start | bytes 7864320 | tf_op jit(solution)/shard_map/all_gather | solution.py:158
  234.9 90.1 %copy-start.64 = (f32[512]{0:T(512)}, f32[512]{0:T(512)S(1)}, u32[]{:S(2)}) copy-start(f32[512]{0:T(512)S(1)} %add_rsqrt_fusion.2) | copy-start | bytes 6148
  241.7 156.5 %reduce-scatter.17.cloned.1.call-start = ((), (), s32[]{:S(2)}) async-start(), calls=%async_computation.13 | async-start | bytes 1966080 | tf_op jit(solution)/shard_map/reduce_scatter | solution.py:204
  321.2 3.8 copy-start.6
  321.2 3.8 copy-start.11
  321.2 3.8 copy-start.12
  321.2 4.2 copy-start.26
  329.1 8.0 %copy-start.21 = (bf16[512,192]{0,1:T(8,128)(2,1)}, bf16[512,192]{0,1:T(8,128)(2,1)S(1)}, u32[]{:S(2)}) copy-start(bf16[512,192]{0,1:T(8,128)(2,1)S(1)} %convolution_convert_fusion.1) | copy-start | bytes 589828
  337.1 72.7 %reduce-scatter.21.cloned.1.call-start = ((), (), s32[]{:S(2)}) async-start(), calls=%async_computation.15 | async-start | bytes 1966080 | tf_op jit(solution)/shard_map/reduce_scatter | solution.py:204
  339.0 8.2 %copy-start.23 = (bf16[512,192]{0,1:T(8,128)(2,1)}, bf16[512,192]{0,1:T(8,128)(2,1)S(1)}, u32[]{:S(2)}) copy-start(bf16[512,192]{0,1:T(8,128)(2,1)S(1)} %convolution_convert_fusion) | copy-start | bytes 589828
  347.2 99.2 %reduce-scatter.19.cloned.1.call-start = ((), (), s32[]{:S(2)}) async-start(), calls=%async_computation.14 | async-start | bytes 1966080 | tf_op jit(solution)/shard_map/reduce_scatter | solution.py:201
  354.7 6.5 copy-start.41
  361.2 3.2 copy-start.2
  364.4 118.6 %reduce-scatter.15.cloned.1.call-start = ((), (), s32[]{:S(2)}) async-start(), calls=%async_computation.12 | async-start | bytes 1966080 | tf_op jit(solution)/shard_map/reduce_scatter | solution.py:201
  371.9 6.5 copy-start.39
  378.4 3.2 copy-start.3
  381.6 225.0 %all-reduce.8.cloned.1.call-start = ((), (), s32[]{:S(2)}) async-start(), calls=%async_computation.24 | async-start | bytes 12582912 | tf_op jit(solution)/shard_map/psum | solution.py:146
  381.9 4.2 copy-start.74
  381.9 13.6 %slice-start = ((s8[6291456]{0:T(1024)(128)(4,1)}), s8[4194304]{0:T(1024)(128)(4,1)S(1)}, s32[]{:S(2)}) async-start(s8[6291456]{0:T(1024)(128)(4,1)} %bitcast.225), calls=%async_computation.27 | async-start | bytes 8388608
  386.0 3.8 copy-start.18
  386.0 9.4 %slice-start.1 = ((s8[6291456]{0:T(1024)(128)(4,1)}), s8[2097152]{0:T(1024)(128)(4,1)S(1)}, s32[]{:S(2)}) async-start(s8[6291456]{0:T(1024)(128)(4,1)} %bitcast.225), calls=%async_computation.28 | async-start | bytes 4194304
  389.8 5.6 copy-start.20
  399.2 84.8 %copy-start.44 = (bf16[1,512,192]{1,2,0:T(8,128)(2,1)}, bf16[1,512,192]{1,2,0:T(8,128)(2,1)S(1)}, u32[]{:S(2)}) copy-start(bf16[1,512,192]{1,2,0:T(8,128)(2,1)S(1)} %convert_bitcast_fusion.6) | copy-start | bytes 589828
  410.8 40.5 %copy-start.46 = (bf16[1,512,192]{1,2,0:T(8,128)(2,1)}, bf16[1,512,192]{1,2,0:T(8,128)(2,1)S(1)}, u32[]{:S(2)}) copy-start(bf16[1,512,192]{1,2,0:T(8,128)(2,1)S(1)} %convert_bitcast_fusion.4) | copy-start | bytes 589828
  488.0 123.6 %reduce-scatter.27.cloned.1.call-start = ((), (), s32[]{:S(2)}) async-start(), calls=%async_computation.20 | async-start | bytes 3538944 | tf_op jit(solution)/shard_map/reduce_scatter | solution.py:243
  488.6 2.7 copy-start.33
  493.8 117.8 %reduce-scatter.29.cloned.1.call-start = ((), (), s32[]{:S(2)}) async-start(), calls=%async_computation.21 | async-start | bytes 3538944 | tf_op jit(solution)/shard_map/reduce_scatter | solution.py:244
  493.9 3.0 copy-start.27
  493.9 3.0 copy-start.78
  499.5 2.8 copy-start.37
  499.5 112.2 %reduce-scatter.25.cloned.1.call-start = ((), (), s32[]{:S(2)}) async-start(), calls=%async_computation.19 | async-start | bytes 884736 | tf_op jit(solution)/shard_map/reduce_scatter | solution.py:242
  503.6 109.4 %reduce-scatter.23.cloned.1.call-start = ((), (), s32[]{:S(2)}) async-start(), calls=%async_computation.18 | async-start | bytes 2654208 | tf_op jit(solution)/shard_map/reduce_scatter | solution.py:241
  508.1 120.6 %reduce-scatter.33.cloned.1.call-start = ((), (), s32[]{:S(2)}) async-start(), calls=%async_computation.23 | async-start | bytes 589824
  511.6 3.3 copy-start.69
  511.6 3.3 copy-start.68
  511.6 95.0 %copy-start.63 = (f32[512]{0:T(512)S(1)}, f32[512]{0:T(512)}, u32[]{:S(2)}) copy-start(f32[512]{0:T(512)} %copy-done.61) | copy-start | bytes 6148
  610.5 34.2 %reduce-scatter.31.cloned.1.call-start = ((), (), s32[]{:S(2)}) async-start(), calls=%async_computation.22 | async-start | bytes 589824
  611.5 169.5 %all-reduce.12.cloned.1.call-start = ((), (), s32[]{:S(2)}) async-start(), calls=%async_computation.26 | async-start | bytes 7077888 | tf_op jit(solution)/shard_map/psum | solution.py:237
  613.0 4.3 copy-start.13
  613.0 4.3 copy-start.14
  781.0 3.0 copy-start.29
  (35 other events, 58.2 us)
Sparse Core Ops, SparseCore 0:
  138.7 69.2 all-reduce.9
  221.7 46.4 all-gather.16
  270.3 46.3 all-gather.14
  488.1 118.4 all-reduce.7
Sparse Core Ops, SparseCore 1:
  140.6 23.4 all-gather.10
  165.5 22.6 all-gather.12
  337.2 35.4 reduce-scatter.16
  375.6 34.2 reduce-scatter.20
  412.1 34.2 reduce-scatter.18
  448.7 34.2 reduce-scatter.14
  493.9 33.5 reduce-scatter.26
  529.6 34.7 reduce-scatter.28
  567.0 15.3 reduce-scatter.24
  584.7 28.2 reduce-scatter.22
  615.6 13.1 reduce-scatter.32
  631.6 13.1 reduce-scatter.30
  647.3 133.7 all-reduce.11
